TPU v7x, 32 devices: a whole 2x2x4 slice. The times are simulated.
32 devices in a mesh: section: 2 (over core), ctx: 16 (over z, y, x).
Axes of the slice: x: 2, y: 2, z: 4, core: 2. Of those that a mesh axis runs over, the one named last changes fastest.
Arguments:
- tokens: bfloat16 [2, 2048, 2048], P(None, 'ctx'), may hold values from -6 to 6
- qkv_weight: bfloat16 [2, 2048, 3072], P('section', 'ctx'), may hold values from -0.125 to 0.125
- out_weight: bfloat16 [2, 1024, 2048], P('section', 'ctx'), may hold values from -0.1875 to 0.1875
- log_decay: float32 [2, 2, 2048, 16], P('section', None, 'ctx'), may hold values from -1.5 to 0, as said below
Outputs:
- hidden_states: bfloat16 [2, 2, 2048, 2048], P('section', None, 'ctx')
Inputs may be any that keep to these rules, and one draw needn't show every extreme that they name: `log_decay`: every value is negative.
All inputs are finite; a program needn't handle non-finite values.
Results may differ from a plain program's by a relative error of at most 0.025.
Values may be sent and summed in bfloat16 or wider, within the bound.
A program may use at most 128 MiB of HBM per device.

v0:
```python
import jax
import jax.numpy as jnp
from jax import lax
from jax.sharding import PartitionSpec as P


def passed_along(value, axis, by):
    devices = lax.axis_size(axis)
    pairs = [(i, i + by) for i in range(devices) if 0 <= i + by < devices]
    return lax.ppermute(value, axis, pairs)


def entering(value, axis, join, neutral):
    place = lax.axis_index(axis)
    gathered = jax.tree.map(
        lambda a, kind: lax.all_gather(a.astype(kind), axis), value, (jnp.bfloat16, jnp.bfloat16)
    )
    state = jax.tree.map(lambda a, e: jnp.zeros_like(a) + jnp.asarray(e, a.dtype), value, neutral)

    def one(hop, state):
        return join(
            state,
            jax.tree.map(
                lambda a, own: lax.dynamic_index_in_dim(a, hop, 0, False).astype(own.dtype),
                gathered,
                value,
            ),
        )

    return lax.fori_loop(0, place, one, state)


def normalize_rows(value_rows):
    return value_rows * lax.rsqrt(jnp.mean(value_rows * value_rows, axis=-1, keepdims=True) + 1e-05)


def local_terms(incoming, weight_full, decay):
    row_count = incoming.shape[0]
    head_count = decay.shape[1]
    normed = normalize_rows(incoming.astype(jnp.float32)).astype(jnp.bfloat16)
    projected = jnp.dot(normed, weight_full, preferred_element_type=jnp.float32).astype(
        jnp.bfloat16
    )
    inner = projected.shape[1] // 3
    head_dim = inner // head_count
    query_rows = projected[:, :inner].reshape(row_count, head_count, head_dim)
    key_block = projected[:, inner : 2 * inner].reshape(row_count, head_count, head_dim)
    value_rows = projected[:, 2 * inner :].reshape(row_count, head_count, head_dim)
    cumulative = jnp.cumsum(decay, axis=0)
    ending = cumulative[-1]
    key_rows_scaled = (
        key_block.astype(jnp.float32) * jnp.exp(ending[None, :] - cumulative)[:, :, None]
    ).astype(jnp.bfloat16)
    block_state = jnp.einsum(
        "yao,yau->aou", key_rows_scaled, value_rows, preferred_element_type=jnp.float32
    )
    return (query_rows, key_block, value_rows, cumulative, block_state, jnp.exp(ending))


def block_attention(query_rows, key_block, value_rows, cumulative):
    row_count = query_rows.shape[0]
    scores = jnp.einsum("thk,jhk->htj", query_rows, key_block, preferred_element_type=jnp.float32)
    per_head = cumulative.T
    decay_gap = per_head[:, :, None] - per_head[:, None, :]
    position_index = jnp.arange(row_count, dtype=jnp.int32)
    causal = position_index[:, None] >= position_index[None, :]
    weights = jnp.where(causal, scores * jnp.exp(jnp.where(causal, decay_gap, 0.0)), 0.0).astype(
        jnp.bfloat16
    )
    return jnp.einsum("htj,jhv->thv", weights, value_rows, preferred_element_type=jnp.float32)


def combine_states(earlier, later):
    return (earlier[0] * later[0], later[0][:, None, None] * earlier[1] + later[1])


def shards(tokens, qkv_weight, out_weight, log_decay):
    sections = lax.axis_size("section")
    section_id = lax.axis_index("section")
    weight_full, out_full = (
        lax.all_gather(qkv_weight[0], "ctx", axis=0, tiled=True),
        lax.all_gather(out_weight[0], "ctx", axis=0, tiled=True),
    )
    micro_count, row_count, model_width = tokens.shape
    head_count = log_decay.shape[3]
    inner = qkv_weight.shape[2] // 3
    head_dim = inner // head_count
    buffer = jnp.zeros((micro_count, row_count, model_width), jnp.bfloat16)
    previous = jnp.zeros((row_count, model_width), jnp.bfloat16)
    for time_step in range(micro_count + sections - 1):
        if time_step > 0:
            received = passed_along(previous, "section", 1)
        else:
            received = jnp.zeros((row_count, model_width), jnp.bfloat16)
        micro_index = time_step - section_id
        active = jnp.logical_and(micro_index >= 0, micro_index < micro_count)
        mb_clip = jnp.clip(micro_index, 0, micro_count - 1)
        own_input = lax.dynamic_index_in_dim(tokens, mb_clip, 0, keepdims=False)
        incoming = jnp.where(section_id == 0, own_input, received)
        decay = lax.dynamic_index_in_dim(log_decay[0], mb_clip, 0, keepdims=False)
        query_rows, key_block, value_rows, cumulative, block_state, block_total = local_terms(
            incoming, weight_full, decay
        )
        intra_out = block_attention(query_rows, key_block, value_rows, cumulative)
        identity = (
            jnp.ones((head_count,), jnp.float32),
            jnp.zeros((head_count, head_dim, head_dim), jnp.float32),
        )
        prefix_total, carried = entering(
            (block_total, block_state), "ctx", combine_states, identity
        )
        carried_state_low = carried.astype(jnp.bfloat16)
        inter_out = (
            jnp.einsum(
                "npc,pco->npo", query_rows, carried_state_low, preferred_element_type=jnp.float32
            )
            * jnp.exp(cumulative)[:, :, None]
        )
        mixture = intra_out + inter_out
        mixed_low = normalize_rows(mixture).reshape(row_count, inner).astype(jnp.bfloat16)
        mixed = jnp.dot(mixed_low, out_full, preferred_element_type=jnp.float32)
        result = (incoming.astype(jnp.float32) + mixed).astype(jnp.bfloat16)
        current_row = lax.dynamic_index_in_dim(buffer, mb_clip, 0, keepdims=False)
        buffer = lax.dynamic_update_index_in_dim(
            buffer, jnp.where(active, result, current_row), mb_clip, 0
        )
        previous = result
    return buffer[None]


def solution(mesh):
    in_specs = (
        P(None, "ctx", None),
        P("section", "ctx", None),
        P("section", "ctx", None),
        P("section", None, "ctx", None),
    )
    out_specs = P("section", None, "ctx", None)
    return jax.shard_map(shards, mesh=mesh, in_specs=in_specs, out_specs=out_specs, check_vma=False)
```

profile of v0, /device:TPU:30, one launch (start us, length us, event | category | flops | bytes accessed | tf_op | source)
XLA Modules:
  0.0 555.6 jit_solution(1691061310572981918)
XLA Ops:
  8.5 1.3 fusion.64
  9.8 149.8 %all-gather.14.cloned.1.call-done = bf16[1,2048,3072]{2,1,0:T(8,128)(2,1)} async-done(((bf16[1,128,3072]{2,1,0:T(8,128)(2,1)}), bf16[1,2048,3072]{2,1,0:T(8,128)(2,1)}) %all-gather.14.cloned.1.call-update) | async-done | bytes 12582928 | tf_op jit(solution)/shard_map/all_gather | solution.py:81
  159.6 6.7 %fusion.12 = bf16[128,3072]{1,0:T(8,128)(2,1)S(1)} fusion(bf16[1,2048,3072]{2,1,0:T(8,128)(2,1)} %all-gather.14.cloned.1.call-done, f32[128]{0:T(128)S(1)} %add_rsqrt_fusion.5, bf16[2,128,2048]{2,1,0:T(8,128)(2,1)} %param.10, s32[]{:T(128)S(6)} %min.10, pred[]{:T(512)S(6)} %eq.2), kind=kOutput, calls=%fused_computation.18 | convolution fusion | flops 1612054528 | bytes 13894149 | tf_op jit(solution)/shard_map/dot_general | solution.py:41
  168.5 35.5 %all-gather.5 = bf16[16,1,16]{2,1,0:T(2,128)(2,1)S(1)} all-gather(bf16[1,1,16]{2,1,0:T(2,128)(2,1)S(1)} %get-tuple-element.194), channel_id=1, replica_groups=mesh['section'=2,'ctx'=16] {'ctx'}, dimensions={0}, use_global_device_ids=true | all-gather | bytes 544 | tf_op jit(solution)/shard_map/all_gather | solution.py:16
  205.2 37.0 %all-gather.16.cloned.1.call-done = bf16[256,64,64]{2,1,0:T(8,128)(2,1)} async-done(((bf16[16,64,64]{2,1,0:T(8,128)(2,1)}), bf16[256,64,64]{2,1,0:T(8,128)(2,1)}) %all-gather.16.cloned.1.call-update) | async-done | bytes 2097168 | tf_op jit(solution)/shard_map/all_gather | solution.py:16
  242.2 17.5 %while.36 = (s32[]{:T(128)}, f32[16,64,64]{2,1,0:T(8,128)S(1)}, s32[]{:T(128)}, bf16[16,16]{1,0:T(8,128)(2,1)S(1)}, bf16[16,16,64,64]{3,2,1,0:T(8,128)(2,1)}, /*index=5*/s32[]{:T(128)}, s32[]{:T(128)}, s32[]{:T(128)}) while((s32[]{:T(128)}, f32[16,64,64]{2,1,0:T(8,128)S(1)}, s32[]{:T(128)}, bf16[16,16]{1,0:T(8,128)(2,1)S(1)}, ...), condition=%wide.region_3.4_spmd, body=%wide.region_2.3_spmd.sunk | while | flops 196629 | bytes 655647 | solution.py:30
  242.2 1.2 convert_add_fusion.6
  243.5 1.1 convert_add_fusion.6
  244.6 1.1 convert_add_fusion.6
  252.7 1.1 convert_add_fusion.6
  253.9 1.1 convert_add_fusion.6
  255.1 1.1 convert_add_fusion.6
  257.4 1.1 convert_add_fusion.6
  258.6 1.1 convert_add_fusion.6
  260.1 59.0 %all-gather.18.cloned.1.call-done = bf16[1,1024,2048]{2,1,0:T(8,128)(2,1)} async-done(((bf16[1,64,2048]{2,1,0:T(8,128)(2,1)}), bf16[1,1024,2048]{2,1,0:T(8,128)(2,1)}) %all-gather.18.cloned.1.call-update) | async-done | bytes 4194320 | tf_op jit(solution)/shard_map/all_gather | solution.py:82
  319.2 3.7 bitcast_dynamic-update-slice_fusion.1
  323.0 1.3 collective-permute-start
  326.3 6.5 %fusion.15 = bf16[128,3072]{1,0:T(8,128)(2,1)S(1)} fusion(bf16[1,2048,3072]{2,1,0:T(8,128)(2,1)} %all-gather.14.cloned.1.call-done, bf16[128,2048]{1,0:T(8,128)(2,1)S(1)} %get-tuple-element.173, f32[128]{0:T(128)S(1)} %add_rsqrt_fusion.4), kind=kOutput, calls=%fused_computation.19 | convolution fusion | flops 1611792384 | bytes 13894144 | tf_op jit(solution)/shard_map/dot_general | solution.py:41
  335.0 35.4 %all-gather.6 = bf16[16,1,16]{2,1,0:T(2,128)(2,1)S(1)} all-gather(bf16[1,1,16]{2,1,0:T(2,128)(2,1)} %get-tuple-element.190), channel_id=1, replica_groups=mesh['section'=2,'ctx'=16] {'ctx'}, dimensions={0}, use_global_device_ids=true | all-gather | bytes 544 | tf_op jit(solution)/shard_map/all_gather | solution.py:16
  371.9 1.1 copy.69
  373.0 2.3 convolution_bitcast_fusion.3
  375.4 33.8 %all-gather.20.cloned.1.call-done = bf16[256,64,64]{2,1,0:T(8,128)(2,1)} async-done(((bf16[16,64,64]{2,1,0:T(8,128)(2,1)}), bf16[256,64,64]{2,1,0:T(8,128)(2,1)}) %all-gather.20.cloned.1.call-update) | async-done | bytes 2097168 | tf_op jit(solution)/shard_map/all_gather | solution.py:16
  409.3 27.3 %while.37 = (s32[]{:T(128)}, f32[16,64,64]{2,1,0:T(8,128)S(1)}, s32[]{:T(128)}, bf16[16,16]{1,0:T(8,128)(2,1)}, bf16[16,16,64,64]{3,2,1,0:T(8,128)(2,1)}, /*index=5*/s32[]{:T(128)}, s32[]{:T(128)}, s32[]{:T(128)}) while((s32[]{:T(128)}, f32[16,64,64]{2,1,0:T(8,128)S(1)}, s32[]{:T(128)}, bf16[16,16]{1,0:T(8,128)(2,1)}, ...), condition=%wide.region_8.9_spmd, body=%wide.region_7.8_spmd.sunk | while | flops 196629 | bytes 655647 | solution.py:30
  436.5 1.3 multiply_reduce_fusion.1
  437.9 3.9 bitcast_dynamic-update-slice_fusion
  441.8 1.5 collective-permute-start.1
  443.7 1.1 collective-permute-done.1
  445.2 6.5 %fusion.18 = bf16[128,3072]{1,0:T(8,128)(2,1)S(1)} fusion(bf16[1,2048,3072]{2,1,0:T(8,128)(2,1)} %all-gather.14.cloned.1.call-done, bf16[128,2048]{1,0:T(8,128)(2,1)S(1)} %get-tuple-element.171, f32[128]{0:T(128)S(1)} %add_rsqrt_fusion.3), kind=kOutput, calls=%fused_computation.20 | convolution fusion | flops 1611792384 | bytes 13894144 | tf_op jit(solution)/shard_map/dot_general | solution.py:41
  453.1 35.2 %all-gather.7 = bf16[16,1,16]{2,1,0:T(2,128)(2,1)S(1)} all-gather(bf16[1,1,16]{2,1,0:T(2,128)(2,1)S(1)} %get-tuple-element.186), channel_id=1, replica_groups=mesh['section'=2,'ctx'=16] {'ctx'}, dimensions={0}, use_global_device_ids=true | all-gather | bytes 544 | tf_op jit(solution)/shard_map/all_gather | solution.py:16
  490.4 37.0 %all-gather.22.cloned.1.call-done = bf16[256,64,64]{2,1,0:T(8,128)(2,1)} async-done(((bf16[16,64,64]{2,1,0:T(8,128)(2,1)}), bf16[256,64,64]{2,1,0:T(8,128)(2,1)}) %all-gather.22.cloned.1.call-update) | async-done | bytes 2097168 | tf_op jit(solution)/shard_map/all_gather | solution.py:16
  527.5 17.4 %while.38 = (s32[]{:T(128)}, f32[16,64,64]{2,1,0:T(8,128)S(1)}, s32[]{:T(128)}, bf16[16,16]{1,0:T(8,128)(2,1)S(1)}, bf16[16,16,64,64]{3,2,1,0:T(8,128)(2,1)}, /*index=5*/s32[]{:T(128)}, s32[]{:T(128)}, s32[]{:T(128)}) while((s32[]{:T(128)}, f32[16,64,64]{2,1,0:T(8,128)S(1)}, s32[]{:T(128)}, bf16[16,16]{1,0:T(8,128)(2,1)S(1)}, ...), condition=%wide.region_13.14_spmd, body=%wide.region_12.13_spmd.sunk | while | flops 196629 | bytes 655647 | solution.py:30
  545.3 3.8 fusion.45
  (160 shorter events, 67.6 us)
Async XLA Ops:
  6.5 153.1 %all-gather.14.cloned.1.call-start = ((), (), s32[]{:S(2)}) async-start(), calls=%async_computation | async-start | bytes 13369344 | tf_op jit(solution)/shard_map/all_gather | solution.py:81
  7.3 234.9 %all-gather.16.cloned.1.call-start = ((), (), s32[]{:S(2)}) async-start(), calls=%async_computation.1 | async-start | bytes 4456448 | tf_op jit(solution)/shard_map/all_gather | solution.py:16
  167.7 151.4 %all-gather.18.cloned.1.call-start = ((), (), s32[]{:S(2)}) async-start(), calls=%async_computation.2 | async-start | bytes 4456448 | tf_op jit(solution)/shard_map/all_gather | solution.py:82
  168.4 240.8 %all-gather.20.cloned.1.call-start = ((), (), s32[]{:S(2)}) async-start(), calls=%async_computation.3 | async-start | bytes 4456448 | tf_op jit(solution)/shard_map/all_gather | solution.py:16
  204.1 38.0 %copy-start.1 = (pred[128,128]{1,0:T(8,128)(4,1)}, pred[128,128]{1,0:T(8,128)(4,1)S(1)}, u32[]{:S(2)}) copy-start(pred[128,128]{1,0:T(8,128)(4,1)S(1)} %iota_compare_fusion) | copy-start | bytes 49156
  242.2 77.0 %copy-start = (bf16[2,128,2048]{2,1,0:T(8,128)(2,1)S(1)}, bf16[2,128,2048]{2,1,0:T(8,128)(2,1)}, u32[]{:S(2)}) copy-start(bf16[2,128,2048]{2,1,0:T(8,128)(2,1)} %param.10) | copy-start | bytes 3145732
  323.0 3.0 collective-permute-start
  334.9 192.6 %all-gather.22.cloned.1.call-start = ((), (), s32[]{:S(2)}) async-start(), calls=%async_computation.4 | async-start | bytes 4456448 | tf_op jit(solution)/shard_map/all_gather | solution.py:16
  441.8 3.0 collective-permute-start.1
  451.7 38.0 %copy-start.2 = (pred[128,128]{1,0:T(8,128)(4,1)S(1)}, pred[128,128]{1,0:T(8,128)(4,1)}, u32[]{:S(2)}) copy-start(pred[128,128]{1,0:T(8,128)(4,1)} %copy-done.1) | copy-start | bytes 49156
Sparse Core Ops, SparseCore 0:
  10.1 149.4 all-gather.13
  167.8 74.2 all-gather.15
  244.9 74.1 all-gather.17
  335.0 74.1 all-gather.19
  453.2 74.2 all-gather.21
where the time goes:
time: 558 us; the launch traced here: 556 us
  waiting for transfers between devices  320 us (57%)
  blocking collectives  106 us (19%)
  other arithmetic  63.9 us (11%)
  matrix products  39.9 us (7%)
  between operations  13.5 us (2%)
  local copies, waits for them, and re-layouts  7.65 us (1%)
    all_gather x1, waiting for transfers between devices, shards(): lax.all_gather(qkv_weight[0], 'ctx', axis=0, tiled=True)  150 us
    all_gather x3, waiting for transfers between devices, entering(): lax.all_gather(a.astype(kind), axis)  108 us
    all_gather x3, blocking collectives, entering(): lax.all_gather(a.astype(kind), axis)  106 us
    all_gather x1, waiting for transfers between devices, shards(): lax.all_gather(out_weight[0], 'ctx', axis=0, tiled=True)  59 us
    add x45, other arithmetic, combine_states(): later[0][:, None, None] * earlier[1] + later[1]  50 us
    dot_general x3, matrix products, local_terms(): jnp.dot(normed, weight_full, preferred_element_type=jnp.float32)  19.7 us
    dot_general x3, matrix products, shards(): mixed = jnp.dot(mixed_low, out_full, preferred_element_type=jnp.float32)  11.4 us
  transfers between devices with their start and end apart: 7, of which 7 were waited for; matrix products, arithmetic and copies ran while one was open for 5% of the time, Pallas kernels for 0%

commit v1 on v0

v1 whole, which is shorter than its diff:
```python
import functools

import jax
import jax.numpy as jnp
import numpy as np
from jax import lax
from jax.experimental import pallas as pl
from jax.experimental.pallas import tpu as pltpu
from jax.sharding import PartitionSpec as P

MESH = pl.DeviceIdType.MESH
TILE = 16


def line_sizes(mesh):
    total = mesh.shape["ctx"]
    places = np.moveaxis(mesh.devices, mesh.axis_names.index("ctx"), 0).reshape(total, -1)[:, 0]
    sizes, left = [], total
    try:
        coords = [tuple(d.coords) for d in places]
    except AttributeError:
        coords = None
    if coords is not None:
        step = 1
        while step < total:
            changed = [a != b for a, b in zip(coords[0], coords[step])]
            axis = changed.index(True)
            size = 1
            while step * size < total and (
                size == 1 or (coords[step * size][axis] != coords[0][axis]
                and all(coords[step * size][i] == coords[0][i] for i in range(3) if i != axis))
            ):
                size += 1
            while total % (step * size):
                size -= 1
            sizes.insert(0, size)
            step *= size
    else:
        while left > 1:
            sizes.append(2)
            left //= 2
    return tuple(sizes)


def routes(sizes):
    d = len(sizes)
    if d != 3:
        return [(tuple(range(d)), 1)]
    return [((0, 2, 1), 3), ((0, 1, 2), 3), ((2, 1, 0), 1), ((1, 2, 0), 1)]


def pieces(rows, sizes):
    orders = routes(sizes)
    units = rows // TILE
    if len(orders) == 1 or units < 2:
        return [(orders[0][0], 0, rows)]
    shares = [units // 2, units - units // 2] if units < 8 else None
    if shares is None:
        whole = sum(s for _, s in orders)
        shares = [s * units // whole for _, s in orders]
        shares[0] += units - sum(shares)
    out, at = [], 0
    for (order, _), share in zip(orders, shares):
        out.append((order, at * TILE, share * TILE))
        at += share
    return out


def place_in_line(me, size, t):
    low = jnp.minimum(me, size - 1 - me)
    half = lax.div(t + 1, 2)
    near = jnp.where(lax.rem(t, 2) == 1, me + half, me - half)
    far = jnp.where(me < size - 1 - me, me + (t - low), me - (t - low))
    return jnp.where(t <= 2 * low, near, far)


def gather_kernel(sizes, plan, *refs):
    count = len(plan)
    shards, wholes = refs[:count], refs[count : 2 * count]
    send_sem, recv_sem, own_sem = refs[2 * count :]
    d = len(sizes)
    total = int(np.prod(sizes))
    strides = [int(np.prod(sizes[i + 1 :])) for i in range(d)]
    me = lax.axis_index("ctx")
    mine = [lax.rem(lax.div(me, strides[i]), sizes[i]) for i in range(d)]
    slots, ways = 0, []
    for i in range(d):
        for sign in (1, -1):
            ways.append((i, sign, slots if sizes[i] == 2 or sign == 1 else slots + 1))
        slots += 1 if sizes[i] == 2 else 2

    barrier = pltpu.get_barrier_semaphore()
    near = jnp.int32(0)
    for i, sign, _ in ways:
        there = jnp.logical_and(mine[i] + sign >= 0, mine[i] + sign < sizes[i])
        near = near + there.astype(jnp.int32)

        @pl.when(there)
        def _(i=i, sign=sign):
            pl.semaphore_signal(
                barrier, inc=1, device_id={"ctx": me + sign * strides[i]}, device_id_type=MESH
            )

    pl.semaphore_wait(barrier, near)

    parts = [(a, order, at, rows) for a in range(count) for order, at, rows in plan[a]]

    def copy(source, index, way, own):
        a, _, at, rows = parts[index]
        i, sign, slot = way
        depth = shards[a].shape[0]
        begin = pl.multiple_of(source * depth + at, TILE)
        target = wholes[a].at[pl.ds(begin, rows)]
        return pltpu.make_async_remote_copy(
            src_ref=shards[a].at[pl.ds(at, rows)] if own else target,
            dst_ref=target,
            send_sem=send_sem.at[source, index, slot],
            recv_sem=recv_sem.at[source, index],
            device_id={"ctx": me + sign * strides[i]},
            device_id_type=MESH,
        )

    def onward(source, coords, index, own, act):
        order = parts[index][1]
        for way in ways:
            i, sign, _ = way
            ok = jnp.logical_and(mine[i] + sign >= 0, mine[i] + sign < sizes[i])
            if not own:
                here = coords[i]
                ok = jnp.logical_and(ok, (mine[i] - here) * sign >= 0)
                for later in order[order.index(i) + 1 :]:
                    ok = jnp.logical_and(ok, mine[later] == coords[later])

            @pl.when(ok)
            def _(way=way):
                act(copy(source, index, way, own))

    for index in range(len(parts)):
        onward(me, mine, index, True, lambda c: c.start())
    own_copies = []
    for a in range(count):
        depth = shards[a].shape[0]
        own_copies.append(
            pltpu.make_async_copy(
                shards[a],
                wholes[a].at[pl.ds(pl.multiple_of(me * depth, TILE), depth)],
                own_sem.at[a],
            )
        )
        own_copies[-1].start()

    def source_of(j):
        coords = [
            place_in_line(mine[i], sizes[i], lax.rem(lax.div(j, strides[i]), sizes[i]))
            for i in range(d)
        ]
        source = sum(c * s for c, s in zip(coords, strides))
        return source, coords

    @pl.loop(1, total)
    def _(j):
        source, coords = source_of(j)
        for index in range(len(parts)):
            copy(source, index, ways[0], False).wait_recv()
            onward(source, coords, index, False, lambda c: c.start())

    for c in own_copies:
        c.wait()
    for index in range(len(parts)):
        onward(me, mine, index, True, lambda c: c.wait_send())

    @pl.loop(1, total)
    def _(j):
        source, coords = source_of(j)
        for index in range(len(parts)):
            onward(source, coords, index, False, lambda c: c.wait_send())


def gather_weights(sizes, *shards):
    total = int(np.prod(sizes))
    plan = [pieces(s.shape[0], sizes) for s in shards]
    parts = sum(len(p) for p in plan)
    slots = sum(1 if s == 2 else 2 for s in sizes)
    return pl.pallas_call(
        functools.partial(gather_kernel, sizes, plan),
        out_shape=[jax.ShapeDtypeStruct((s.shape[0] * total, s.shape[1]), s.dtype) for s in shards],
        in_specs=[pl.BlockSpec(memory_space=pl.ANY)] * len(shards),
        out_specs=[pl.BlockSpec(memory_space=pl.ANY)] * len(shards),
        scratch_shapes=[
            pltpu.SemaphoreType.DMA((total, parts, slots)),
            pltpu.SemaphoreType.DMA((total, parts)),
            pltpu.SemaphoreType.DMA((len(shards),)),
        ],
        compiler_params=pltpu.CompilerParams(collective_id=0, has_side_effects=True),
        name="gather_weights",
    )(*shards)


def carry_kernel(total, rows, send_ref, out_ref, got, carried, landed, s1, r1, s2, r2):
    me = lax.axis_index("ctx")
    barrier = pltpu.get_barrier_semaphore()

    @pl.loop(1, total)
    def _(k):
        pl.semaphore_signal(
            barrier, inc=1, device_id={"ctx": lax.rem(me + k, total)}, device_id_type=MESH
        )

    pl.semaphore_wait(barrier, total - 1)

    def first(to, slot_from):
        return pltpu.make_async_remote_copy(
            src_ref=send_ref.at[to],
            dst_ref=got.at[slot_from],
            send_sem=s1.at[to],
            recv_sem=r1.at[slot_from],
            device_id={"ctx": to},
            device_id_type=MESH,
        )

    def second(to, slot_from):
        return pltpu.make_async_remote_copy(
            src_ref=carried.at[to],
            dst_ref=landed.at[slot_from],
            send_sem=s2.at[to],
            recv_sem=r2.at[slot_from],
            device_id={"ctx": to},
            device_id_type=MESH,
        )

    @pl.loop(1, total)
    def _(k):
        first(lax.rem(me + k, total), me).start()

    got[me] = send_ref[me]

    def step(b, acc):
        @pl.when(b != me)
        def _():
            first(b, b).wait_recv()

        low = acc.astype(jnp.bfloat16)
        carried[b] = low

        @pl.when(b != me)
        def _():
            second(b, me).start()

        @pl.when(b == me)
        def _():
            landed[me] = low

        item = got[b].astype(jnp.float32)
        return acc * item[rows : rows + 1] + item[:rows]

    lax.fori_loop(0, total, step, jnp.zeros((rows, out_ref.shape[2]), jnp.float32))

    @pl.loop(1, total)
    def _(k):
        peer = lax.rem(me + k, total)
        first(peer, me).wait_send()
        second(peer, me).wait_send()
        second(peer, peer).wait_recv()

    out_ref[...] = landed[...]


def carry(total, items, call_id):
    rows = items.shape[1] - TILE
    lanes = items.shape[2]
    return pl.pallas_call(
        functools.partial(carry_kernel, total, rows),
        out_shape=jax.ShapeDtypeStruct((total, rows, lanes), jnp.bfloat16),
        in_specs=[pl.BlockSpec(memory_space=pltpu.VMEM)],
        out_specs=pl.BlockSpec(memory_space=pltpu.VMEM),
        scratch_shapes=[
            pltpu.VMEM((total, rows + TILE, lanes), jnp.bfloat16),
            pltpu.VMEM((total, rows, lanes), jnp.bfloat16),
            pltpu.VMEM((total, rows, lanes), jnp.bfloat16),
            pltpu.SemaphoreType.DMA((total,)),
            pltpu.SemaphoreType.DMA((total,)),
            pltpu.SemaphoreType.DMA((total,)),
            pltpu.SemaphoreType.DMA((total,)),
        ],
        compiler_params=pltpu.CompilerParams(collective_id=1, has_side_effects=True),
        name="carry_states",
    )(items)


def normalize_rows(value_rows):
    return value_rows * lax.rsqrt(jnp.mean(value_rows * value_rows, axis=-1, keepdims=True) + 1e-05)


def layer(total, incoming, weight_full, out_full, decay):
    micro, row_count, model_width = incoming.shape
    heads = decay.shape[2]
    wide = incoming.astype(jnp.float32)
    normed = normalize_rows(wide).astype(jnp.bfloat16).reshape(micro * row_count, model_width)
    projected = jnp.dot(normed, weight_full, preferred_element_type=jnp.float32).astype(
        jnp.bfloat16
    )
    inner = projected.shape[1] // 3
    head_dim = inner // heads
    q = projected[:, :inner].reshape(micro, row_count, heads, head_dim)
    k = projected[:, inner : 2 * inner].reshape(micro, row_count, heads, head_dim)
    v = projected[:, 2 * inner :].reshape(micro, row_count, heads, head_dim)
    cumul = jnp.cumsum(decay, axis=1)
    ending = cumul[:, -1]
    scaled = (k.astype(jnp.float32) * jnp.exp(ending[:, None, :] - cumul)[..., None]).astype(
        jnp.bfloat16
    )
    state = jnp.einsum("mthk,mthv->mhkv", scaled, v, preferred_element_type=jnp.float32)
    rows = heads * head_dim // total
    flat = state.astype(jnp.bfloat16).transpose(1, 2, 0, 3).reshape(total, rows, micro * head_dim)
    totals = jnp.exp(ending).astype(jnp.bfloat16)
    totals = jnp.broadcast_to(
        totals.T[:, None, :, None], (heads, head_dim, micro, head_dim)
    ).reshape(total, rows, micro * head_dim)[:, :1]
    items = jnp.concatenate(
        [flat, jnp.broadcast_to(totals, (total, TILE, micro * head_dim))], axis=1
    )
    low = carry(total, items, 1)
    carried = low.reshape(heads, head_dim, micro, head_dim)
    scores = jnp.einsum("mthk,mjhk->mhtj", q, k, preferred_element_type=jnp.float32)
    per_head = cumul.transpose(0, 2, 1)
    gap = per_head[..., :, None] - per_head[..., None, :]
    at = jnp.arange(row_count, dtype=jnp.int32)
    causal = at[:, None] >= at[None, :]
    weights = jnp.where(causal, scores * jnp.exp(jnp.where(causal, gap, 0.0)), 0.0).astype(
        jnp.bfloat16
    )
    intra = jnp.einsum("mhtj,mjhv->mthv", weights, v, preferred_element_type=jnp.float32)
    inter = (
        jnp.einsum("mthk,hkmv->mthv", q, carried, preferred_element_type=jnp.float32)
        * jnp.exp(cumul)[..., None]
    )
    mixed = normalize_rows(intra + inter).reshape(micro * row_count, inner).astype(jnp.bfloat16)
    product = jnp.dot(mixed, out_full, preferred_element_type=jnp.float32)
    return (wide + product.reshape(micro, row_count, model_width)).astype(jnp.bfloat16)


def shards(sizes, tokens, qkv_weight, out_weight, log_decay):
    sections = lax.axis_size("section")
    total = lax.axis_size("ctx")
    section_id = lax.axis_index("section")
    weight_full, out_full = gather_weights(sizes, qkv_weight[0], out_weight[0])
    result = tokens
    kept = tokens
    for stage in range(sections):
        result = layer(total, result, weight_full, out_full, log_decay[0])
        kept = jnp.where(section_id == stage, result, kept)
        if stage < sections - 1:
            result = lax.ppermute(
                result, "section", [(i, i + 1) for i in range(sections - 1)]
            )
    return kept[None]


def solution(mesh):
    in_specs = (
        P(None, "ctx", None),
        P("section", "ctx", None),
        P("section", "ctx", None),
        P("section", None, "ctx", None),
    )
    out_specs = P("section", None, "ctx", None)
    return jax.shard_map(
        functools.partial(shards, line_sizes(mesh)),
        mesh=mesh,
        in_specs=in_specs,
        out_specs=out_specs,
        check_vma=False,
    )
```

time: 558 us -> 263 us (0.47)
  the two profiles are of different devices: /device:TPU:30 before, /device:TPU:1 now
where the time goes in v1:
time: 263 us; the launch traced here: 259 us
  Pallas kernels  178 us (68%)
  matrix products  38.7 us (15%)
  local copies, waits for them, and re-layouts  22.8 us (9%)
  waiting for transfers between devices  9.85 us (4%)
  other arithmetic  8.68 us (3%)
    pallas_call x1, Pallas kernels, gather_weights(): pl.pallas_call(functools.partial(gather_kernel, sizes, plan), out_shape=[...  135 us
    pallas_call x2, Pallas kernels, carry(): pl.pallas_call(functools.partial(carry_kernel, total, rows), out_shape=ja...  42.9 us
    dot_general x2, matrix products, layer(): jnp.dot(normed, weight_full, preferred_element_type=jnp.float32)  16 us
    ppermute x1, waiting for transfers between devices, shards(): lax.ppermute(result, 'section', [(i, i + 1) for i in range(sections - 1)])  9.85 us
    dot_general x2, matrix products, layer(): product = jnp.dot(mixed, out_full, preferred_element_type=jnp.float32)  8.1 us
    dot_general x2, matrix products, layer(): jnp.einsum('mhtj,mjhv->mthv', weights, v, preferred_element_type=jnp.floa...  7.44 us
    reshape x4, local copies, waits for them, and re-layouts, layer(): q = projected[:, :inner].reshape(micro, row_count, heads, head_dim)  6.96 us
  transfers between devices with their start and end apart: 1, of which 1 were waited for; matrix products, arithmetic and copies ran while one was open for 0% of the time, Pallas kernels for 0%

profile of v1, /device:TPU:1, one launch (start us, length us, event | category | flops | bytes accessed | tf_op | source)
XLA Modules:
  0.0 259.3 jit_solution(2890773563349461149)
XLA Ops:
  0.0 0.9 copy.28
  1.3 1.5 fusion.20
  3.0 134.8 %gather_weights.1 = (bf16[2048,3072]{1,0:T(8,128)(2,1)}, bf16[1024,2048]{1,0:T(8,128)(2,1)}) custom-call(bf16[128,3072]{1,0:T(8,128)(2,1)} %bitcast.73, bf16[64,2048]{1,0:T(8,128)(2,1)} %bitcast.74), custom_call_target="tpu_custom_call" | custom-call | tf_op jit(solution)/shard_map/gather_weights/pallas_call | solution.py:184
  137.9 8.0 %convolution_convert_fusion.1 = bf16[256,3072]{1,0:T(8,128)(2,1)S(1)} fusion(bf16[256,2048]{1,0:T(8,128)(2,1)S(1)} %bitcast.71, bf16[2048,3072]{1,0:T(8,128)(2,1)} %get-tuple-element.7), kind=kOutput, calls=%fused_computation.5 | convolution fusion | flops 3222011904 | bytes 15204352 | tf_op jit(solution)/shard_map/dot_general | solution.py:299
  145.9 0.9 fusion.54
  147.8 0.9 copy.31
  151.5 24.0 %carry_states.2 = bf16[16,64,128]{2,1,0:T(8,128)(2,1)} custom-call(bf16[16,80,128]{2,1,0:T(8,128)(2,1)} %pad_maximum_fusion.1.send_ref), custom_call_target="tpu_custom_call" | custom-call | tf_op jit(solution)/shard_map/carry_states/pallas_call | solution.py:271
  175.5 2.0 reshape.96
  177.5 1.9 reshape.104
  179.5 1.6 copy.38
  181.2 2.6 fusion.31
  183.8 3.6 %multiply_reduce_fusion.1 = (f32[2,128,16]{1,2,0:T(8,128)S(1)}, f32[2,128,16,64]{1,3,2,0:T(8,128)}) fusion(f32[2,128,16,64]{1,3,2,0:T(8,128)} %fusion.31, bf16[2,128,16,64]{1,3,2,0:T(8,128)(2,1)S(1)} %copy.31, bf16[2,128,16,64]{1,3,2,0:T(8,128)(2,1)S(1)} %copy-done.6, f32[2,16,128]{2,1,0:T(8,128)S(1)} %copy.29, pred[128,128]{1,0:T(8,128)(4,1)S(1)} %iota_compare_fusion, ...), kind=kOutput, calls=%fused_computation.41 | convolution fusion | flops 137621504 | bytes 3719168 | tf_op jit(solution)/shard_map/mhtj,mjhv->mthv/dot_general | solution.py:332
  187.4 1.4 multiply_convert_fusion.2
  188.8 3.5 %fusion.8 = bf16[2,128,2048]{2,1,0:T(8,128)(2,1)S(1)} fusion(bf16[2,128,1024]{1,2,0:T(8,128)(2,1)S(1)} %bitcast.69, bf16[1024,2048]{1,0:T(8,128)(2,1)} %get-tuple-element.8, bf16[2,128,2048]{2,1,0:T(8,128)(2,1)S(1)} %copy-done), kind=kOutput, calls=%fused_computation.12 | convolution fusion | flops 1075314688 | bytes 6815744 | tf_op jit(solution)/shard_map/dot_general | solution.py:338
  192.3 1.3 collective-permute-start
  193.6 9.9 %collective-permute-done = bf16[2,128,2048]{2,1,0:T(8,128)(2,1)S(1)} collective-permute-done((bf16[2,128,2048]{2,1,0:T(8,128)(2,1)S(1)}, bf16[2,128,2048]{2,1,0:T(8,128)(2,1)S(1)}, u32[]{:S(2)}, u32[]{:S(2)}) %collective-permute-start) | collective-permute-done | bytes 1048608 | tf_op jit(solution)/shard_map/ppermute | solution.py:353
  204.0 8.0 %convolution_convert_fusion = bf16[256,3072]{1,0:T(8,128)(2,1)S(1)} fusion(bf16[256,2048]{1,0:T(8,128)(2,1)S(1)} %bitcast.72, bf16[2048,3072]{1,0:T(8,128)(2,1)} %get-tuple-element.7), kind=kOutput, calls=%fused_computation.4 | convolution fusion | flops 3222011904 | bytes 15204352 | tf_op jit(solution)/shard_map/dot_general | solution.py:299
  212.0 1.2 fusion.53
  213.2 1.2 copy.43
  214.6 1.3 multiply_convert_fusion.1
  215.9 1.8 reshape.107
  217.7 1.6 copy.44
  219.3 1.6 fusion.33
  221.7 0.7 pad_maximum_fusion.send_ref
  222.5 18.9 %carry_states.3 = bf16[16,64,128]{2,1,0:T(8,128)(2,1)} custom-call(bf16[16,80,128]{2,1,0:T(8,128)(2,1)} %pad_maximum_fusion.send_ref), custom_call_target="tpu_custom_call" | custom-call | tf_op jit(solution)/shard_map/carry_states/pallas_call | solution.py:271
  241.3 2.0 reshape.102
  243.4 1.8 reshape.105
  245.1 1.6 copy.49
  246.7 2.6 %fusion.30 = f32[2,128,16,64]{1,3,2,0:T(8,128)} fusion(bf16[2,128,16,64]{1,3,2,0:T(8,128)(2,1)} %copy.49, bf16[16,64,2,64]{3,2,1,0:T(2,128)(2,1)} %reshape.102, f32[2,128,16]{1,2,0:T(8,128)S(1)} %copy.39), kind=kOutput, calls=%fused_computation.30 | convolution fusion | flops 33816576 | bytes 1851392 | tf_op jit(solution)/shard_map/mthk,hkmv->mthv/dot_general | solution.py:334
  249.4 3.8 %multiply_reduce_fusion = (f32[2,128,16]{1,2,0:T(8,128)S(1)}, f32[2,128,16,64]{1,3,2,0:T(8,128)}) fusion(f32[2,128,16,64]{1,3,2,0:T(8,128)} %fusion.30, bf16[2,128,16,64]{1,3,2,0:T(8,128)(2,1)S(1)} %copy-done.3, bf16[2,128,16,64]{1,3,2,0:T(8,128)(2,1)} %copy.49, f32[2,16,128]{2,1,0:T(8,128)S(1)} %copy.29, pred[128,128]{1,0:T(8,128)(4,1)S(1)} %iota_compare_fusion, ...), kind=kOutput, calls=%fused_computation.38 | convolution fusion | flops 137621504 | bytes 3719168 | tf_op jit(solution)/shard_map/mhtj,mjhv->mthv/dot_general | solution.py:332
  253.2 1.4 multiply_convert_fusion
  254.7 4.6 %fusion.17 = bf16[1,2,128,2048]{3,2,1,0:T(8,128)(2,1)} fusion(bf16[2,128,1024]{1,2,0:T(8,128)(2,1)S(1)} %bitcast.68, bf16[1024,2048]{1,0:T(8,128)(2,1)} %get-tuple-element.8, bf16[2,128,2048]{2,1,0:T(8,128)(2,1)S(1)} %collective-permute-done, bf16[2,128,2048]{2,1,0:T(8,128)(2,1)S(1)} %copy-done.2, bf16[2,128,2048]{2,1,0:T(8,128)(2,1)S(1)} %copy-done, ...), kind=kOutput, calls=%fused_computation.15 | convolution fusion | flops 1076363264 | bytes 8912898 | tf_op jit(solution)/shard_map/dot_general | solution.py:338
  (44 shorter events, 6.0 us)
Async XLA Ops:
  0.0 2.8 %copy-start = (bf16[2,128,2048]{2,1,0:T(8,128)(2,1)S(1)}, bf16[2,128,2048]{2,1,0:T(8,128)(2,1)}, u32[]{:S(2)}) copy-start(bf16[2,128,2048]{2,1,0:T(8,128)(2,1)} %param.4) | copy-start | bytes 3145732
  181.1 2.6 %copy-start.6 = (bf16[2,128,16,64]{1,3,2,0:T(8,128)(2,1)S(1)}, bf16[2,128,16,64]{1,3,2,0:T(8,128)(2,1)}, u32[]{:S(2)}) copy-start(bf16[2,128,16,64]{1,3,2,0:T(8,128)(2,1)} %copy.38) | copy-start | bytes 1572868
  192.3 19.7 %copy-start.1 = (bf16[2,128,2048]{2,1,0:T(8,128)(2,1)}, bf16[2,128,2048]{2,1,0:T(8,128)(2,1)S(1)}, u32[]{:S(2)}) copy-start(bf16[2,128,2048]{2,1,0:T(8,128)(2,1)S(1)} %fusion.8) | copy-start | bytes 3145732
  192.3 11.2 %collective-permute-start = (bf16[2,128,2048]{2,1,0:T(8,128)(2,1)S(1)}, bf16[2,128,2048]{2,1,0:T(8,128)(2,1)S(1)}, u32[]{:S(2)}, u32[]{:S(2)}) collective-permute-start(bf16[2,128,2048]{2,1,0:T(8,128)(2,1)S(1)} %fusion.8), channel_id=1, source_target_pairs={{0,16},{1,17},{2,18},{3,19},{4,20},{5,21},{6,22},{7,23},{8,24},{9,... | collective-permute-start | bytes 3145736 | tf_op jit(solution)/shard_map/ppermute | solution.py:353
  214.6 1.3 copy-start.4
  246.7 2.6 %copy-start.3 = (bf16[2,128,16,64]{1,3,2,0:T(8,128)(2,1)S(1)}, bf16[2,128,16,64]{1,3,2,0:T(8,128)(2,1)}, u32[]{:S(2)}) copy-start(bf16[2,128,16,64]{1,3,2,0:T(8,128)(2,1)} %copy.44) | copy-start | bytes 1572868
  246.7 2.6 %copy-start.5 = (bf16[2,128,16,64]{1,0,3,2:T(2,128)(2,1)S(1)}, bf16[2,128,16,64]{1,0,3,2:T(2,128)(2,1)}, u32[]{:S(2)}) copy-start(bf16[2,128,16,64]{1,0,3,2:T(2,128)(2,1)} %copy-done.4) | copy-start | bytes 1572868
  253.2 1.5 copy-start.2

commit v2 on v1

v2 whole, which is shorter than its diff:
```python
import functools

import jax
import jax.numpy as jnp
import numpy as np
from jax import lax
from jax.experimental import pallas as pl
from jax.experimental.pallas import tpu as pltpu
from jax.sharding import PartitionSpec as P

MESH = pl.DeviceIdType.MESH
TILE = 16


def line_sizes(mesh):
    total = mesh.shape["ctx"]
    places = np.moveaxis(mesh.devices, mesh.axis_names.index("ctx"), 0).reshape(total, -1)[:, 0]
    sizes, left = [], total
    try:
        coords = [tuple(d.coords) for d in places]
    except AttributeError:
        coords = None
    if coords is not None:
        step = 1
        while step < total:
            changed = [a != b for a, b in zip(coords[0], coords[step])]
            axis = changed.index(True)
            size = 1
            while step * size < total and (
                size == 1 or (coords[step * size][axis] != coords[0][axis]
                and all(coords[step * size][i] == coords[0][i] for i in range(3) if i != axis))
            ):
                size += 1
            while total % (step * size):
                size -= 1
            sizes.insert(0, size)
            step *= size
    else:
        while left > 1:
            sizes.append(2)
            left //= 2
    return tuple(sizes)


def routes(sizes):
    d = len(sizes)
    if d != 3:
        return [(tuple(range(d)), 1)]
    return [((0, 2, 1), 3), ((0, 1, 2), 3), ((2, 1, 0), 1), ((1, 2, 0), 1)]


def pieces(rows, sizes):
    orders = routes(sizes)
    units = rows // TILE
    if len(orders) == 1 or units < 2:
        return [(orders[0][0], 0, rows)]
    shares = [units // 2, units - units // 2] if units < 8 else None
    if shares is None:
        whole = sum(s for _, s in orders)
        shares = [s * units // whole for _, s in orders]
        shares[0] += units - sum(shares)
    out, at = [], 0
    for (order, _), share in zip(orders, shares):
        out.append((order, at * TILE, share * TILE))
        at += share
    return out


def place_in_line(me, size, t):
    low = jnp.minimum(me, size - 1 - me)
    half = lax.div(t + 1, 2)
    near = jnp.where(lax.rem(t, 2) == 1, me + half, me - half)
    far = jnp.where(me < size - 1 - me, me + (t - low), me - (t - low))
    return jnp.where(t <= 2 * low, near, far)


def dot(a, b, contract=((1,), (0,)), precision=None):
    return lax.dot_general(
        a, b, (contract, ((), ())), precision=precision, preferred_element_type=jnp.float32
    )


def whole_kernel(
    sizes, sections, plan, heads, tokens, decay, shard_a, shard_b, out,
    full_a, full_b, xbuf, normed, proj, cumx, cumt, intra, mixed, result, items, got, carried,
    landed, send_sem, recv_sem, own_sem, x_send, x_recv, start_sem, s1, r1, s2, r2,
):
    f32, bf16 = jnp.float32, jnp.bfloat16
    shards, wholes = (shard_a, shard_b), (full_a, full_b)
    count = 2
    d = len(sizes)
    total = int(np.prod(sizes))
    strides = [int(np.prod(sizes[i + 1 :])) for i in range(d)]
    me = lax.axis_index("ctx")
    section = lax.axis_index("section")
    mine = [lax.rem(lax.div(me, strides[i]), sizes[i]) for i in range(d)]
    slots, ways = 0, []
    for i in range(d):
        for sign in (1, -1):
            ways.append((i, sign, slots if sizes[i] == 2 or sign == 1 else slots + 1))
        slots += 1 if sizes[i] == 2 else 2
    micro, rows, width = xbuf.shape
    inner = mixed.shape[1]
    head_dim = inner // heads
    pairs = heads // 2
    lanes = 2 * head_dim
    part = items.shape[1] - TILE

    barrier = pltpu.get_barrier_semaphore()

    @pl.loop(1, total)
    def _(k):
        pl.semaphore_signal(
            barrier, inc=1, device_id={"ctx": lax.rem(me + k, total)}, device_id_type=MESH
        )

    @pl.when(section > 0)
    def _():
        pl.semaphore_signal(barrier, inc=1, device_id={"section": section - 1}, device_id_type=MESH)

    @pl.when(section < sections - 1)
    def _():
        pl.semaphore_signal(barrier, inc=1, device_id={"section": section + 1}, device_id_type=MESH)

    greeted = (section > 0).astype(jnp.int32) + (section < sections - 1).astype(jnp.int32)
    pl.semaphore_wait(barrier, greeted + (total - 1))

    parts = [(a, order, at, size) for a in range(count) for order, at, size in plan[a]]

    def copy(source, index, way, own):
        a, _, at, size = parts[index]
        i, sign, slot = way
        depth = shards[a].shape[0]
        begin = pl.multiple_of(source * depth + at, TILE)
        target = wholes[a].at[pl.ds(begin, size)]
        return pltpu.make_async_remote_copy(
            src_ref=shards[a].at[pl.ds(at, size)] if own else target,
            dst_ref=target,
            send_sem=send_sem.at[source, index, slot],
            recv_sem=recv_sem.at[source, index],
            device_id={"ctx": me + sign * strides[i]},
            device_id_type=MESH,
        )

    def onward(source, coords, index, own, act):
        order = parts[index][1]
        for way in ways:
            i, sign, _ = way
            ok = jnp.logical_and(mine[i] + sign >= 0, mine[i] + sign < sizes[i])
            if not own:
                here = coords[i]
                ok = jnp.logical_and(ok, (mine[i] - here) * sign >= 0)
                for later in order[order.index(i) + 1 :]:
                    ok = jnp.logical_and(ok, mine[later] == coords[later])

            @pl.when(ok)
            def _(way=way):
                act(copy(source, index, way, own))

    own_copies = []
    for a in range(count):
        depth = shards[a].shape[0]
        own_copies.append(
            pltpu.make_async_copy(
                shards[a],
                wholes[a].at[pl.ds(pl.multiple_of(me * depth, TILE), depth)],
                own_sem.at[a],
            )
        )
        own_copies[-1].start()

    x_own = pltpu.make_async_copy(tokens, xbuf, own_sem.at[2])

    @pl.when(section == 0)
    def _():
        x_own.start()

    @pl.when(section > 0)
    def _():
        pl.semaphore_wait(start_sem, 1)

    for index in range(len(parts)):
        onward(me, mine, index, True, lambda c: c.start())

    at_row = lax.broadcasted_iota(jnp.int32, (rows, rows), 0)
    at_col = lax.broadcasted_iota(jnp.int32, (rows, rows), 1)
    causal = at_row >= at_col
    lower = causal.astype(f32)
    for m in range(micro):
        spread = (
            lax.broadcasted_iota(jnp.int32, (heads, heads * lanes), 0)
            == lax.broadcasted_iota(jnp.int32, (heads, heads * lanes), 1) // lanes
        ).astype(f32)
        own = decay[m]
        summed = dot(lower, own, precision=lax.Precision.HIGHEST)
        cumx[m] = dot(summed, spread, precision=lax.Precision.HIGHEST)
        cumt[m] = dot(own.T, lower, ((1,), (1,)), precision=lax.Precision.HIGHEST)

    def source_of(j):
        coords = [
            place_in_line(mine[i], sizes[i], lax.rem(lax.div(j, strides[i]), sizes[i]))
            for i in range(d)
        ]
        source = sum(c * s for c, s in zip(coords, strides))
        return source, coords

    @pl.loop(1, total)
    def _(j):
        source, coords = source_of(j)
        for index in range(len(parts)):
            copy(source, index, ways[0], False).wait_recv()
            onward(source, coords, index, False, lambda c: c.start())

        @pl.when(jnp.logical_and(j == total - GATE, section < sections - 1))
        def _():
            pl.semaphore_signal(
                start_sem, inc=1, device_id={"section": section + 1}, device_id_type=MESH
            )

    for c in own_copies:
        c.wait()

    pass_on = pltpu.make_async_remote_copy(
        src_ref=result,
        dst_ref=xbuf,
        send_sem=x_send.at[0],
        recv_sem=x_recv.at[0],
        device_id={"section": lax.rem(section + 1, sections)},
        device_id_type=MESH,
    )

    @pl.when(section == 0)
    def _():
        x_own.wait()

    @pl.when(section > 0)
    def _():
        pass_on.wait_recv()

    for m in range(micro):

        @pl.loop(0, rows // TILE)
        def _(r, m=m):
            at = pl.multiple_of(r * TILE, TILE)
            wide = xbuf[m, pl.ds(at, TILE), :].astype(f32)
            scale = lax.rsqrt(jnp.mean(wide * wide, axis=-1, keepdims=True) + 1e-05)
            normed[pl.ds(pl.multiple_of(m * rows + at, TILE), TILE), :] = (wide * scale).astype(bf16)

    @pl.loop(0, 3 * inner // 256)
    def _(c):
        cols = pl.ds(pl.multiple_of(c * 256, 256), 256)
        proj[:, cols] = dot(normed[...], full_a[:, cols]).astype(bf16)

    first_half = lax.broadcasted_iota(jnp.int32, (rows, lanes), 1) < head_dim
    first_item = lax.broadcasted_iota(jnp.int32, (head_dim, lanes), 1) < head_dim
    per_pair = head_dim // part

    def located(u):
        m, p = lax.div(u, pairs), lax.rem(u, pairs)
        span = pl.ds(pl.multiple_of(m * rows, TILE), rows)

        def column(which):
            return pl.ds(pl.multiple_of(which * inner + p * lanes, lanes), lanes)

        def cum(h):
            return cumx[m, :, pl.ds(pl.multiple_of((2 * p + h) * lanes, lanes), lanes)]

        return m, p, span, column, cum

    @pl.loop(0, micro * pairs)
    def _(u):
        m, p, span, column, cum = located(u)
        both = jnp.where(first_half, cum(0), cum(1))
        ending = both[rows - 1 :, :]
        scaled = (proj[span, column(1)].astype(f32) * jnp.exp(ending - both)).astype(bf16)
        state = dot(scaled, proj[span, column(2)], ((0,), (0,)))
        packed = jnp.where(first_item, state[:head_dim], state[head_dim:]).astype(bf16)
        weight = jnp.broadcast_to(jnp.exp(ending), (TILE, lanes)).astype(bf16)
        for piece in range(per_pair):
            items[u * per_pair + piece, :part, :] = packed[piece * part : (piece + 1) * part]
            items[u * per_pair + piece, part:, :] = weight

    def first(to, slot_from):
        return pltpu.make_async_remote_copy(
            src_ref=items.at[to],
            dst_ref=got.at[slot_from],
            send_sem=s1.at[to],
            recv_sem=r1.at[slot_from],
            device_id={"ctx": to},
            device_id_type=MESH,
        )

    def second(to, slot_from):
        return pltpu.make_async_remote_copy(
            src_ref=carried.at[to],
            dst_ref=landed.at[slot_from],
            send_sem=s2.at[to],
            recv_sem=r2.at[slot_from],
            device_id={"ctx": to},
            device_id_type=MESH,
        )

    @pl.loop(1, total)
    def _(k):
        first(lax.rem(me + k, total), me).start()

    got[me] = items[me]

    @pl.loop(0, micro * pairs)
    def _(u):
        m, p, span, column, cum = located(u)
        queries, keys, values = (proj[span, column(i)] for i in range(3))
        outs = []
        for h in range(2):
            own_half = first_half if h == 0 else jnp.logical_not(first_half)
            scores = dot(jnp.where(own_half, queries, jnp.zeros_like(queries)), keys, ((1,), (1,)))
            gap = cum(h) - cumt[m, pl.ds(2 * p + h, 1), :]
            weights = jnp.where(
                causal, scores * jnp.exp(jnp.where(causal, gap, 0.0)), 0.0
            ).astype(bf16)
            outs.append(dot(weights, values))
        intra[span, column(0)] = jnp.where(first_half, outs[0], outs[1])

    def step(b, acc):
        @pl.when(b != me)
        def _():
            first(b, b).wait_recv()

        low = acc.astype(bf16)
        carried[b] = low

        @pl.when(b != me)
        def _():
            second(b, me).start()

        @pl.when(b == me)
        def _():
            landed[me] = low

        item = got[b].astype(f32)
        return acc * item[part : part + 1] + item[:part]

    lax.fori_loop(0, total, step, jnp.zeros((part, lanes), f32))

    @pl.loop(1, total)
    def _(k):
        peer = lax.rem(me + k, total)
        second(peer, peer).wait_recv()

    @pl.loop(0, micro * pairs)
    def _(u):
        m, p, span, column, cum = located(u)
        low = jnp.concatenate([landed[u * per_pair + i] for i in range(per_pair)], axis=0)
        none = jnp.zeros_like(low)
        block = jnp.concatenate(
            [jnp.where(first_item, low, none), jnp.where(first_item, none, low)], axis=0
        )
        both = jnp.where(first_half, cum(0), cum(1))
        mixture = intra[span, column(0)] + dot(proj[span, column(0)], block) * jnp.exp(both)
        squares = mixture * mixture
        scales = [
            lax.rsqrt(
                jnp.sum(jnp.where(own, squares, 0.0), axis=-1, keepdims=True) / head_dim + 1e-05
            )
            for own in (first_half, jnp.logical_not(first_half))
        ]
        mixed[span, column(0)] = (mixture * jnp.where(first_half, scales[0], scales[1])).astype(bf16)

    @pl.loop(0, width // 256)
    def _(c):
        cols = pl.ds(pl.multiple_of(c * 256, 256), 256)
        product = dot(mixed[...], full_b[:, cols])
        for m in range(micro):
            result[m, :, cols] = (
                xbuf[m, :, cols].astype(f32) + product[m * rows : (m + 1) * rows]
            ).astype(bf16)

    @pl.when(section < sections - 1)
    def _():
        pass_on.start()

    put = pltpu.make_async_copy(result, out, own_sem.at[3])
    put.start()

    for index in range(len(parts)):
        onward(me, mine, index, True, lambda c: c.wait_send())

    @pl.loop(1, total)
    def _(j):
        source, coords = source_of(j)
        for index in range(len(parts)):
            onward(source, coords, index, False, lambda c: c.wait_send())

    @pl.loop(1, total)
    def _(k):
        peer = lax.rem(me + k, total)
        first(peer, me).wait_send()
        second(peer, me).wait_send()

    put.wait()

    @pl.when(section < sections - 1)
    def _():
        pass_on.wait_send()


GATE = 1


def shards(sizes, sections, tokens, qkv_weight, out_weight, log_decay):
    micro, rows, width = tokens.shape
    total = int(np.prod(sizes))
    heads = log_decay.shape[3]
    own = (qkv_weight[0], out_weight[0])
    inner = own[1].shape[0] * total
    lanes = 2 * inner // heads
    part = micro * inner // 2 // total
    plan = [pieces(s.shape[0], sizes) for s in own]
    count = sum(len(p) for p in plan)
    slots = sum(1 if s == 2 else 2 for s in sizes)
    f32, bf16 = jnp.float32, jnp.bfloat16
    dma = pltpu.SemaphoreType.DMA
    anywhere = pl.BlockSpec(memory_space=pl.ANY)
    vmem = pl.BlockSpec(memory_space=pltpu.VMEM)
    result = pl.pallas_call(
        functools.partial(whole_kernel, sizes, sections, plan, heads),
        out_shape=jax.ShapeDtypeStruct(tokens.shape, tokens.dtype),
        in_specs=[anywhere, vmem, anywhere, anywhere],
        out_specs=anywhere,
        scratch_shapes=[
            pltpu.VMEM((own[0].shape[0] * total, own[0].shape[1]), bf16),
            pltpu.VMEM((own[1].shape[0] * total, own[1].shape[1]), bf16),
            pltpu.VMEM((micro, rows, width), bf16),
            pltpu.VMEM((micro * rows, width), bf16),
            pltpu.VMEM((micro * rows, 3 * inner), bf16),
            pltpu.VMEM((micro, rows, heads * lanes), f32),
            pltpu.VMEM((micro, heads, rows), f32),
            pltpu.VMEM((micro * rows, inner), f32),
            pltpu.VMEM((micro * rows, inner), bf16),
            pltpu.VMEM((micro, rows, width), bf16),
            pltpu.VMEM((total, part + TILE, lanes), bf16),
            pltpu.VMEM((total, part + TILE, lanes), bf16),
            pltpu.VMEM((total, part, lanes), bf16),
            pltpu.VMEM((total, part, lanes), bf16),
            dma((total, count, slots)),
            dma((total, count)),
            dma((4,)),
            dma((1,)),
            dma((1,)),
            pltpu.SemaphoreType.REGULAR,
            dma((total,)),
            dma((total,)),
            dma((total,)),
            dma((total,)),
        ],
        compiler_params=pltpu.CompilerParams(
            collective_id=0, has_side_effects=True, vmem_limit_bytes=60 * 2**20
        ),
        name="mixer_stack",
    )(tokens, log_decay[0], *own)
    return result[None]


def solution(mesh):
    in_specs = (
        P(None, "ctx", None),
        P("section", "ctx", None),
        P("section", "ctx", None),
        P("section", None, "ctx", None),
    )
    out_specs = P("section", None, "ctx", None)
    return jax.shard_map(
        functools.partial(shards, line_sizes(mesh), mesh.shape["section"]),
        mesh=mesh,
        in_specs=in_specs,
        out_specs=out_specs,
        check_vma=False,
    )
```

time: 263 us -> 206 us (0.78); the launches traced: 259 us -> 206 us
  matrix products: 38.7 us -> 0 us
  Pallas kernels: 178 us -> 202 us
  local copies, waits for them, and re-layouts: 22.8 us -> 3.78 us
  waiting for transfers between devices: 9.85 us -> 0 us
  other arithmetic: 8.68 us -> 0 us
    dot_general x10 -> x0, matrix products: 38.7 us -> none  [the longest x2 16 us: layer(): jnp.dot(normed, weight_full, preferred_element_type=jnp.float32)]
    pallas_call x3 -> x1, Pallas kernels: 178 us -> 202 us  [shards(): pl.pallas_call(functools.partial(whole_kernel, sizes, sections, plan, hea...]
    reshape x14 -> x0, local copies, waits for them, and re-layouts: 16.6 us -> none  [the longest x4 6.96 us: layer(): q = projected[:, :inner].reshape(micro, row_count, heads, head_dim)]
    ppermute x1 -> x0, waiting for transfers between devices: 9.85 us -> none  [shards(): lax.ppermute(result, 'section', [(i, i + 1) for i in range(sections - 1)])]
    convert_element_type x6 -> x0, other arithmetic: 5.09 us -> none  [the longest x2 2.8 us: layer(): normalize_rows(intra + inter).reshape(micro * row_count, inner)]
    unnamed x14 -> x2, local copies, waits for them, and re-layouts: 0.1 us -> 3.78 us
    slice x5 -> x0, local copies, waits for them, and re-layouts: 3.59 us -> none  [the longest x4 3.59 us: layer(): k = projected[:, inner:2 * inner].reshape(micro, row_count, heads, head_dim)]
  transfers between devices with their start and end apart: 1 -> 0, of which waited for: 1 -> 0; matrix products, arithmetic and copies ran while one was open for 0% -> 0% of each run, Pallas kernels for 0% -> 0%
where the time goes in v2:
time: 206 us
  Pallas kernels  202 us (98%)
  local copies, waits for them, and re-layouts  3.78 us (2%)
    pallas_call x1, Pallas kernels, shards(): pl.pallas_call(functools.partial(whole_kernel, sizes, sections, plan, hea...  202 us

profile of v2, /device:TPU:1, one launch (start us, length us, event | category | flops | bytes accessed | tf_op | source)
XLA Modules:
  0.0 205.7 jit_solution(5027356966950046288)
XLA Ops:
  0.0 1.5 copy.5
  1.5 201.9 %mixer_stack.1 = bf16[2,128,2048]{2,1,0:T(8,128)(2,1)} custom-call(bf16[2,128,2048]{2,1,0:T(8,128)(2,1)} %tokens.1, f32[2,128,16]{2,1,0:T(8,128)} %bitcast.6, bf16[128,3072]{1,0:T(8,128)(2,1)} %bitcast.5, bf16[64,2048]{1,0:T(8,128)(2,1)} %bitcast.7), custom_call_target="tpu_custom_call" | custom-call | tf_op jit(solution)/shard_map/mixer_stack/pallas_call | solution.py:425
  203.4 2.3 %copy.7 = bf16[1,2,128,2048]{3,2,1,0:T(8,128)(2,1)} copy(bf16[1,2,128,2048]{3,2,1,0:T(8,128)(2,1)} %bitcast.4) | data formatting | bytes 2097152

commit v3 on v2

--- a/solution.py
+++ b/solution.py
@@ -204,19 +204,45 @@
         source = sum(c * s for c, s in zip(coords, strides))
         return source, coords
 
-    @pl.loop(1, total)
-    def _(j):
-        source, coords = source_of(j)
-        for index in range(len(parts)):
-            copy(source, index, ways[0], False).wait_recv()
-            onward(source, coords, index, False, lambda c: c.start())
-
-        @pl.when(jnp.logical_and(j == total - GATE, section < sections - 1))
+    def receive(wanted, least, most):
+        @pl.loop(least * total, most * total)
+        def _(k):
+            hops, j = lax.div(k, total), lax.rem(k, total)
+            source, coords = source_of(j)
+            away = sum(jnp.abs(mine[i] - coords[i]) for i in range(d))
+
+            @pl.when(away == hops)
+            def _():
+                for index in range(len(parts)):
+                    if parts[index][0] == wanted:
+                        copy(source, index, ways[0], False).wait_recv()
+                        onward(source, coords, index, False, lambda c: c.start())
+
+    farthest = sum(n - 1 for n in sizes) + 1
+
+    def let_next_start():
+        @pl.when(section < sections - 1)
         def _():
             pl.semaphore_signal(
                 start_sem, inc=1, device_id={"section": section + 1}, device_id_type=MESH
             )
 
+    def normalize():
+        @pl.loop(0, micro * (rows // TILE))
+        def _(r):
+            m, q = lax.div(r, rows // TILE), lax.rem(r, rows // TILE)
+            wide = xbuf[m, pl.ds(pl.multiple_of(q * TILE, TILE), TILE), :].astype(f32)
+            scale = lax.rsqrt(jnp.mean(wide * wide, axis=-1, keepdims=True) + 1e-05)
+            normed[pl.ds(pl.multiple_of(r * TILE, TILE), TILE), :] = (wide * scale).astype(bf16)
+
+    @pl.when(section == 0)
+    def _():
+        x_own.wait()
+        normalize()
+
+    receive(0, 1, farthest)
+
+    let_next_start()
     for c in own_copies:
         c.wait()
 
@@ -229,22 +255,11 @@
         device_id_type=MESH,
     )
 
-    @pl.when(section == 0)
-    def _():
-        x_own.wait()
-
     @pl.when(section > 0)
     def _():
+        receive(1, 1, farthest)
         pass_on.wait_recv()
-
-    for m in range(micro):
-
-        @pl.loop(0, rows // TILE)
-        def _(r, m=m):
-            at = pl.multiple_of(r * TILE, TILE)
-            wide = xbuf[m, pl.ds(at, TILE), :].astype(f32)
-            scale = lax.rsqrt(jnp.mean(wide * wide, axis=-1, keepdims=True) + 1e-05)
-            normed[pl.ds(pl.multiple_of(m * rows + at, TILE), TILE), :] = (wide * scale).astype(bf16)
+        normalize()
 
     @pl.loop(0, 3 * inner // 256)
     def _(c):
@@ -306,8 +321,7 @@
 
     got[me] = items[me]
 
-    @pl.loop(0, micro * pairs)
-    def _(u):
+    def within(u):
         m, p, span, column, cum = located(u)
         queries, keys, values = (proj[span, column(i)] for i in range(3))
         outs = []
@@ -321,6 +335,18 @@
             outs.append(dot(weights, values))
         intra[span, column(0)] = jnp.where(first_half, outs[0], outs[1])
 
+    @pl.when(section == 0)
+    def _():
+        receive(1, 1, 2)
+
+    @pl.loop(0, micro * pairs)
+    def _(u):
+        within(u)
+
+    @pl.when(section == 0)
+    def _():
+        receive(1, 2, 3)
+
     def step(b, acc):
         @pl.when(b != me)
         def _():
@@ -341,6 +367,10 @@
         return acc * item[part : part + 1] + item[:part]
 
     lax.fori_loop(0, total, step, jnp.zeros((part, lanes), f32))
+
+    @pl.when(section == 0)
+    def _():
+        receive(1, 3, farthest)
 
     @pl.loop(1, total)
     def _(k):
@@ -402,9 +432,6 @@
     @pl.when(section < sections - 1)
     def _():
         pass_on.wait_send()
-
-
-GATE = 1
 
 
 def shards(sizes, sections, tokens, qkv_weight, out_weight, log_decay):

time: 206 us -> 192 us (0.932)
  Pallas kernels: 202 us -> 188 us
    pallas_call x1, Pallas kernels: 202 us -> 188 us  [shards(): pl.pallas_call(functools.partial(whole_kernel, sizes, sections, plan, hea...]
where the time goes in v3:
time: 192 us; the launch traced here: 191 us
  Pallas kernels  188 us (98%)
  local copies, waits for them, and re-layouts  3.78 us (2%)
    pallas_call x1, Pallas kernels, shards(): pl.pallas_call(functools.partial(whole_kernel, sizes, sections, plan, hea...  188 us

profile of v3, /device:TPU:1, one launch (start us, length us, event | category | flops | bytes accessed | tf_op | source)
XLA Modules:
  0.0 191.5 jit_solution(5778982031911332404)
XLA Ops:
  0.0 1.5 copy.5
  1.5 187.7 %mixer_stack.1 = bf16[2,128,2048]{2,1,0:T(8,128)(2,1)} custom-call(bf16[2,128,2048]{2,1,0:T(8,128)(2,1)} %tokens.1, f32[2,128,16]{2,1,0:T(8,128)} %bitcast.6, bf16[128,3072]{1,0:T(8,128)(2,1)} %bitcast.5, bf16[64,2048]{1,0:T(8,128)(2,1)} %bitcast.7), custom_call_target="tpu_custom_call" | custom-call | tf_op jit(solution)/shard_map/mixer_stack/pallas_call | solution.py:452
  189.2 2.3 %copy.7 = bf16[1,2,128,2048]{3,2,1,0:T(8,128)(2,1)} copy(bf16[1,2,128,2048]{3,2,1,0:T(8,128)(2,1)} %bitcast.4) | data formatting | bytes 2097152
